TPU v7x, 512 devices: a whole 4x4x16 slice. The times are simulated.
512 devices in a mesh: section: 4 (over x), trial: 128 (over z, y, core).
Axes of the slice: x: 4, y: 4, z: 16, core: 2. Of those that a mesh axis runs over, the one named last changes fastest.
Arguments:
- spike_rates: bfloat16 [512, 256, 256], P(None, 'trial'), may hold values from -6 to 6
- first_preactivation: bfloat16 [1024, 256, 256], P('section', 'trial'), may hold values from -6 to 6
- second_preactivation: bfloat16 [1024, 256, 256], P('section', 'trial'), may hold values from -6 to 6
- output_gradient: bfloat16 [1024, 256, 256], P('section', 'trial'), may hold values from -0.29882812 to 0.29882812
- first_kernel: bfloat16 [3, 1024, 1024], P(None, None, 'section'), may hold values from -0.109375 to 0.109375
- second_kernel: bfloat16 [3, 1024, 1024], P(None, None, 'section'), may hold values from -0.109375 to 0.109375
- session_of: int32 [256], P('trial'), may hold values from 0 to 127, never falling along the last dimension, each value on 1 to 6 neighbouring positions
Outputs:
- readin_grad: bfloat16 [128, 512, 1024], P(None, 'trial', 'section')
Inputs may be any that keep to these rules, and one draw needn't show every extreme that they name: `session_of`: the trials of a session are consecutive; every session has 1 to 6 trials, and one has exactly 6.
All inputs are finite; a program needn't handle non-finite values.
Results may differ from a plain program's by a relative error of at most 0.017.
Values may be sent and summed in bfloat16 or wider, within the bound.
No kernel may reach another device: no remote copies, remote signals or barrier semaphores. Data moves between devices by JAX's collectives and lax.ppermute only.
A program may use at most 64 MiB of HBM per device.

v0:
```python
import math
import jax
import jax.numpy as jnp
from jax import lax
from jax.sharding import PartitionSpec as P

FIRST_DILATION = 32
SECOND_DILATION = 64
MOST = 6


def gelu_slope(preact):
    values = preact.astype(jnp.float32)
    normal_cdf = 0.5 * (1.0 + lax.erf(values * (1.0 / math.sqrt(2.0))))
    density = jnp.exp(-0.5 * values * values) * (1.0 / math.sqrt(2.0 * math.pi))
    return normal_cdf + values * density


def shift_ahead(values, offset):
    padding = [(0, 0)] * (values.ndim - 1) + [(0, offset)]
    return jnp.pad(values[..., offset:], padding)


def tap_sum(weights, flow_grad, spacing):
    running = None
    for kernel_tap in range(3):
        term_tap = lax.dot_general(
            weights[kernel_tap],
            flow_grad,
            (((1,), (0,)), ((), ())),
            preferred_element_type=jnp.float32,
        )
        if kernel_tap > 0:
            term_tap = shift_ahead(term_tap, kernel_tap * spacing)
        running = term_tap if running is None else running + term_tap
    return running


def layer_backprop(upstream, preact, turned, spacing):
    flow_grad = (upstream.astype(jnp.float32) * gelu_slope(preact)).astype(jnp.bfloat16)
    back_sum = tap_sum(turned, lax.all_gather(flow_grad, "section", axis=0, tiled=True), spacing)
    return (upstream.astype(jnp.float32) + back_sum).astype(jnp.bfloat16)


def body(
    spike_rates,
    first_preactivation,
    second_preactivation,
    output_gradient,
    first_kernel,
    second_kernel,
    session_of,
):
    first_flipped_kernel, second_flipped_kernel = (
        lax.all_to_all(first_kernel, "section", split_axis=1, concat_axis=2, tiled=True),
        lax.all_to_all(second_kernel, "section", split_axis=1, concat_axis=2, tiled=True),
    )
    upstream_gradient = layer_backprop(
        output_gradient, second_preactivation, second_flipped_kernel, SECOND_DILATION
    )
    input_gradient = layer_backprop(
        upstream_gradient, first_preactivation, first_flipped_kernel, FIRST_DILATION
    )
    trial_shards = lax.axis_size("trial")
    neurons, trials, steps_count = spike_rates.shape
    neuron_blocks = spike_rates.reshape(trial_shards, neurons // trial_shards, trials, steps_count)
    partials = jnp.einsum(
        "jbil,cil->jibc", neuron_blocks, input_gradient, preferred_element_type=jnp.float32
    )
    arrived = lax.all_to_all(
        partials.astype(jnp.bfloat16), "trial", split_axis=0, concat_axis=0, tiled=True
    ).astype(partials.dtype)
    every_id = lax.all_gather(session_of, "trial", axis=0, tiled=True)
    total_trials = every_id.shape[0]
    flat_parts = arrived.reshape(total_trials, -1)
    session_list = jnp.arange(trial_shards, dtype=jnp.int32)
    first_trial = jnp.sum((every_id[None, :] < session_list[:, None]).astype(jnp.int32), axis=1)

    def add_offset(offset, running):
        position = first_trial + offset
        clipped = jnp.minimum(position, total_trials - 1)
        rows_here = jnp.take(flat_parts, clipped, axis=0)
        valid = (position < total_trials) & (jnp.take(every_id, clipped, axis=0) == session_list)
        return running + jnp.where(valid[:, None], rows_here, 0.0)

    start_sums = jnp.zeros((trial_shards, flat_parts.shape[1]), jnp.float32)
    summed = lax.fori_loop(0, MOST, add_offset, start_sums)
    return summed.reshape(trial_shards, neurons // trial_shards, input_gradient.shape[0]).astype(
        jnp.bfloat16
    )


def solution(mesh):
    in_specs = (
        P(None, "trial", None),
        P("section", "trial", None),
        P("section", "trial", None),
        P("section", "trial", None),
        P(None, None, "section"),
        P(None, None, "section"),
        P("trial"),
    )
    out_specs = P(None, "trial", "section")
    return jax.shard_map(body, mesh=mesh, in_specs=in_specs, out_specs=out_specs, check_vma=False)
```

profile of v0, /device:TPU:8, one launch (start us, length us, event | category | flops | bytes accessed | tf_op | source)
XLA Modules:
  0.0 186.1 jit_solution(364001516441620479)
XLA Ops:
  6.5 1.2 copy.50
  7.8 1.1 copy.51
  8.9 1.0 fusion.14
  9.9 2.7 %copy.52 = bf16[3,1024,256]{2,0,1:T(4,128)(2,1)} copy(bf16[3,1024,256]{2,1,0:T(8,128)(2,1)S(1)} %copy-done.3) | data formatting | bytes 3145728 | tf_op args[5]
  12.6 4.4 %all-to-all-start = ((bf16[3,1024,256]{2,0,1:T(4,128)(2,1)}), bf16[3,1024,256]{2,0,1:T(4,128)(2,1)S(1)}, u32[]{:S(2)}, u32[]{:S(2)}) async-start(bf16[3,1024,256]{2,0,1:T(4,128)(2,1)} %copy.52), calls=%async_computation | async-start | bytes 4194304 | tf_op jit(solution)/shard_map/all_to_all | solution.py:56
  17.0 0.2 copy.54
  17.2 29.0 %all-to-all-done = bf16[3,1024,256]{2,0,1:T(4,128)(2,1)S(1)} async-done(((bf16[3,1024,256]{2,0,1:T(4,128)(2,1)}), bf16[3,1024,256]{2,0,1:T(4,128)(2,1)S(1)}, u32[]{:S(2)}, u32[]{:S(2)}) %all-to-all-start) | async-done | bytes 1572896 | tf_op jit(solution)/shard_map/all_to_all | solution.py:56
  46.2 1.5 copy.79
  47.7 0.5 fusion.34
  48.2 0.4 reshape.105
  48.6 0.4 reshape.106
  49.0 0.4 reshape.104
  49.4 6.2 %all-gather.3.cloned.1.call-done = bf16[1024,2,256]{0,2,1:T(8,128)(2,1)} async-done(((bf16[256,2,256]{0,2,1:T(8,128)(2,1)}), bf16[1024,2,256]{0,2,1:T(8,128)(2,1)}) %all-gather.3.cloned.1.call-update) | async-done | bytes 1048592 | tf_op jit(solution)/shard_map/all_gather | solution.py:41
  55.6 1.8 convolution_bitcast_fusion.4
  57.4 0.5 convolution_bitcast_fusion.3
  57.9 1.5 fusion.31
  59.4 1.4 copy.55
  60.8 31.6 %all_to_all.35 = bf16[3,1024,256]{2,0,1:T(4,128)(2,1)S(1)} all-to-all(bf16[3,1024,256]{2,0,1:T(4,128)(2,1)S(1)} %copy.55), channel_id=1, replica_groups=mesh['section'=4,'trial'=128] {'section'}, dimensions={1} | all-to-all | bytes 3145728 | tf_op jit(solution)/shard_map/all_to_all | solution.py:55
  92.3 0.2 copy.56
  92.7 0.2 copy.59
  92.9 0.2 copy.61
  93.1 0.2 copy.57
  93.3 7.2 %all-gather.5.cloned.1.call-done = bf16[1024,2,256]{0,2,1:T(8,128)(2,1)} async-done(((bf16[256,2,256]{0,2,1:T(8,128)(2,1)}), bf16[1024,2,256]{0,2,1:T(8,128)(2,1)}) %all-gather.5.cloned.1.call-update) | async-done | bytes 1048592 | tf_op jit(solution)/shard_map/all_gather | solution.py:41
  100.5 1.8 convolution_bitcast_fusion.1
  102.3 0.4 convolution_bitcast_fusion
  102.8 2.0 %fusion.3 = bf16[128,2,4,256]{0,3,2,1:T(8,128)(2,1)S(1)} fusion(f32[256,2,256]{0,2,1:T(8,128)} %get-tuple-element.154, bf16[1024,2,256]{0,2,1:T(8,128)(2,1)S(1)} %copy-done.1, bf16[256,1024,1]{0,1,2:T(8,128)(2,1)S(1)} %bitcast.90, bf16[128,4,2,256]{3,2,1,0:T(2,128)(2,1)S(1)} %bitcast.84, f32[256,2,192]{0,2,1:T(8,128)S(1)} %slice.59, ...), kind=kOutput, calls=%fused_computation.13 | convolution fusion | flops 403439616 | bytes 3997696 | tf_op jit(solution)/shard_map/jbil,cil->jibc/dot_general | solution.py:67
  104.8 1.2 copy.65
  106.0 19.0 %all-to-all-start.2 = ((bf16[128,2,4,256]{3,2,1,0:T(4,128)(2,1)}), bf16[128,2,4,256]{3,2,1,0:T(4,128)(2,1)S(1)}, u32[]{:S(2)}, u32[]{:S(2)}) async-start(bf16[128,2,4,256]{3,2,1,0:T(4,128)(2,1)} %copy.65), calls=%async_computation.2 | async-start | bytes 1048576 | tf_op jit(solution)/shard_map/all_to_all | solution.py:70
  125.0 1.2 dynamic-slice
  126.8 0.2 dynamic-update-slice
  127.1 37.2 %all-reduce.4 = s32[256]{0:T(256)S(1)} all-reduce(s32[256]{0:T(256)S(1)} %dynamic-update-slice), channel_id=1, replica_groups=mesh['section'=4,'trial'=128] {'trial'}, use_global_device_ids=true, to_apply=%add.4 | all-reduce | flops 256 | bytes 2048
  164.5 13.8 %while.14 = (s32[]{:T(128)}, f32[128,1024]{1,0:T(8,128)S(1)}, s32[128]{0:T(128)S(1)}, s32[256]{0:T(256)S(1)}, f32[256,1024]{1,0:T(8,128)S(1)}, /*index=5*/s32[]{:T(128)}, s32[]{:T(128)}) while((s32[]{:T(128)}, f32[128,1024]{1,0:T(8,128)S(1)}, s32[128]{0:T(128)S(1)}, s32[256]{0:T(256)S(1)}, f32[256,1024]{1,0:T(8,128)S(1)}, ...), condition=%wide.region_2.3_spmd.clone, body=%wide.region_1.2_spmd.clone.sunk | while | flops 527491 | bytes 2630751 | solution.py:87
  164.6 1.3 gather_fusion.1
  165.9 0.8 gather_fusion
  166.7 0.2 select_add_fusion.2
  166.9 1.3 gather_fusion.1
  168.1 0.8 gather_fusion
  169.0 0.2 select_add_fusion.2
  169.2 1.3 gather_fusion.1
  170.4 0.8 gather_fusion
  171.3 0.2 select_add_fusion.2
  171.5 1.3 gather_fusion.1
  172.7 0.8 gather_fusion
  173.7 1.3 gather_fusion.1
  175.0 0.8 gather_fusion
  176.0 1.3 gather_fusion.1
  177.3 0.8 gather_fusion
  178.3 0.9 convert_element_type.61
  (50 shorter events, 1.1 us)
Async XLA Ops:
  6.5 96.3 %copy-start = (bf16[512,2,256]{2,1,0:T(2,128)(2,1)S(1)}, bf16[512,2,256]{2,1,0:T(2,128)(2,1)}, u32[]{:S(2)}) copy-start(bf16[512,2,256]{2,1,0:T(2,128)(2,1)} %param.9) | copy-start | bytes 1572868
  6.5 3.4 %copy-start.3 = (bf16[3,1024,256]{2,1,0:T(8,128)(2,1)S(1)}, bf16[3,1024,256]{2,1,0:T(8,128)(2,1)}, u32[]{:S(2)}) copy-start(bf16[3,1024,256]{2,1,0:T(8,128)(2,1)} %param.14) | copy-start | bytes 4718596
  6.5 49.0 %all-gather.3.cloned.1.call-start = ((), (), s32[]{:S(2)}) async-start(), calls=%async_computation.3 | async-start | bytes 1310720 | tf_op jit(solution)/shard_map/all_gather | solution.py:41
  12.6 4.4 %copy-start.5 = (bf16[256,2,256]{2,1,0:T(2,128)(2,1)S(1)}, bf16[256,2,256]{2,1,0:T(2,128)(2,1)}, u32[]{:S(2)}) copy-start(bf16[256,2,256]{2,1,0:T(2,128)(2,1)} %param.10) | copy-start | bytes 786436
  12.6 33.6 %all-to-all-start = ((bf16[3,1024,256]{2,0,1:T(4,128)(2,1)}), bf16[3,1024,256]{2,0,1:T(4,128)(2,1)S(1)}, u32[]{:S(2)}, u32[]{:S(2)}) async-start(bf16[3,1024,256]{2,0,1:T(4,128)(2,1)} %copy.52), calls=%async_computation | async-start | bytes 4194304 | tf_op jit(solution)/shard_map/all_to_all | solution.py:56
  17.0 83.5 %all-gather.5.cloned.1.call-start = ((), (), s32[]{:S(2)}) async-start(), calls=%async_computation.4 | async-start | bytes 1310720 | tf_op jit(solution)/shard_map/all_gather | solution.py:41
  55.6 1.8 copy-start.2
  57.9 1.5 copy-start.4
  100.5 1.8 copy-start.1
  104.8 22.1 %copy-start.6 = (s32[2]{0:T(128)S(1)}, s32[2]{0:T(128)}, u32[]{:S(2)}) copy-start(s32[2]{0:T(128)} %param.15) | copy-start | bytes 28
  106.0 58.4 %all-to-all-start.2 = ((bf16[128,2,4,256]{3,2,1,0:T(4,128)(2,1)}), bf16[128,2,4,256]{3,2,1,0:T(4,128)(2,1)S(1)}, u32[]{:S(2)}, u32[]{:S(2)}) async-start(bf16[128,2,4,256]{3,2,1,0:T(4,128)(2,1)} %copy.65), calls=%async_computation.2 | async-start | bytes 1048576 | tf_op jit(solution)/shard_map/all_to_all | solution.py:70
Sparse Core Ops, SparseCore 0:
  10.0 45.5 all-gather.2
  59.5 40.9 all-gather.4
where the time goes:
time: 187 us; the launch traced here: 186 us
  blocking collectives  68.8 us (37%)
  waiting for transfers between devices  42.5 us (23%)
  local copies, waits for them, and re-layouts  26.8 us (14%)
  starting transfers between devices  23.4 us (13%)
  between operations  14.2 us (8%)
  matrix products  7.88 us (4%)
  other arithmetic  2.14 us (1%)
    unnamed x1, blocking collectives  37.2 us
    all_to_all x1, blocking collectives, body(): lax.all_to_all(first_kernel, 'section', split_axis=1, concat_axis=2, tile...  31.6 us
    all_to_all x1, waiting for transfers between devices, body(): lax.all_to_all(second_kernel, 'section', split_axis=1, concat_axis=2, til...  29 us
    all_to_all x1, starting transfers between devices, body(): lax.all_to_all(partials.astype(jnp.bfloat16), 'trial', split_axis=0, conc...  19 us
    all_gather x2, waiting for transfers between devices, layer_backprop(): lax.all_gather(flow_grad, 'section', axis=0, tiled=True)  13.4 us
    unnamed x23, local copies, waits for them, and re-layouts  8.19 us
    gather x6, local copies, waits for them, and re-layouts, add_offset(): jnp.take(every_id, clipped, axis=0) == session_list  7.59 us
    dot_general x5, matrix products, tap_sum(): lax.dot_general(weights[kernel_tap], flow_grad, (((1,), (0,)), ((), ())),...  5.91 us
  transfers between devices with their start and end apart: 4, of which 3 were waited for; matrix products, arithmetic and copies ran while one was open for 5% of the time, Pallas kernels for 0%

commit v1 on v0

--- a/solution.py
+++ b/solution.py
@@ -7,6 +7,27 @@
 FIRST_DILATION = 32
 SECOND_DILATION = 64
 MOST = 6
+
+
+def gather_around(shard, axis, dim):
+    devices, mine, width = (lax.axis_size(axis), lax.axis_index(axis), shard.shape[dim])
+    right = [(i, (i + 1) % devices) for i in range(devices)]
+    left = [(i, (i - 1) % devices) for i in range(devices)]
+    out = jnp.zeros((*shard.shape[:dim], devices * width, *shard.shape[dim + 1 :]), shard.dtype)
+    out = lax.dynamic_update_slice_in_dim(out, shard, mine * width, axis=dim)
+    from_left = from_right = shard
+    middle = devices // 2
+    for lap in range(1, middle + 1):
+        from_left = lax.ppermute(from_left, axis, right)
+        out = lax.dynamic_update_slice_in_dim(
+            out, from_left, (mine - lap) % devices * width, axis=dim
+        )
+        if lap < devices - middle:
+            from_right = lax.ppermute(from_right, axis, left)
+            out = lax.dynamic_update_slice_in_dim(
+                out, from_right, (mine + lap) % devices * width, axis=dim
+            )
+    return out
 
 
 def gelu_slope(preact):
@@ -38,7 +59,7 @@
 
 def layer_backprop(upstream, preact, turned, spacing):
     flow_grad = (upstream.astype(jnp.float32) * gelu_slope(preact)).astype(jnp.bfloat16)
-    back_sum = tap_sum(turned, lax.all_gather(flow_grad, "section", axis=0, tiled=True), spacing)
+    back_sum = tap_sum(turned, gather_around(flow_grad, "section", 0), spacing)
     return (upstream.astype(jnp.float32) + back_sum).astype(jnp.bfloat16)
 
 

time: 187 us -> 178 us (0.952)
  blocking collectives: 68.8 us -> 37 us
  starting transfers between devices: 23.4 us -> 46.6 us
  local copies, waits for them, and re-layouts: 26.8 us -> 43.2 us
  between operations: 14.2 us -> 1.09 us
  waiting for transfers between devices: 42.5 us -> 38.5 us
    all_to_all x1 -> x0, blocking collectives: 31.6 us -> none  [body(): lax.all_to_all(first_kernel, 'section', split_axis=1, concat_axis=2, tile...]
    ppermute x0 -> x6, waiting for transfers between devices: none -> 30.5 us  [the longest x4 30.5 us: gather_around(): from_left = lax.ppermute(from_left, axis, right)]
    all_to_all x1, waiting for transfers between devices: 29 us -> 0.01 us  [body(): lax.all_to_all(second_kernel, 'section', split_axis=1, concat_axis=2, til...]
    ppermute x0 -> x6, starting transfers between devices: none -> 18.1 us  [the longest x4 11.7 us: gather_around(): from_left = lax.ppermute(from_left, axis, right)]
    all_gather x2 -> x0, waiting for transfers between devices: 13.4 us -> none  [layer_backprop(): lax.all_gather(flow_grad, 'section', axis=0, tiled=True)]
    all_to_all x0 -> x1, waiting for transfers between devices: none -> 8.03 us  [body(): lax.all_to_all(first_kernel, 'section', split_axis=1, concat_axis=2, tile...]
    dynamic_update_slice x0 -> x6, local copies, waits for them, and re-layouts: none -> 4.89 us  [the longest x4 2.94 us: gather_around(): lax.dynamic_update_slice_in_dim(out, from_left, (mine - lap) % devices *...]
    all_to_all x0 -> x1, starting transfers between devices: none -> 4.46 us  [body(): lax.all_to_all(first_kernel, 'section', split_axis=1, concat_axis=2, tile...]
  transfers between devices with their start and end apart: 4 -> 9, of which waited for: 3 -> 5; matrix products, arithmetic and copies ran while one was open for 5% -> 17% of each run, Pallas kernels for 0% -> 0%
where the time goes in v1:
time: 178 us; the launch traced here: 177 us
  starting transfers between devices  46.6 us (26%)
  local copies, waits for them, and re-layouts  43.2 us (24%)
  waiting for transfers between devices  38.5 us (22%)
  blocking collectives  37 us (21%)
  matrix products  7.5 us (4%)
  other arithmetic  3.11 us (2%)
    unnamed x1, blocking collectives  37 us
    ppermute x4, waiting for transfers between devices, gather_around(): from_left = lax.ppermute(from_left, axis, right)  30.5 us
    all_to_all x1, starting transfers between devices, body(): lax.all_to_all(partials.astype(jnp.bfloat16), 'trial', split_axis=0, conc...  19.5 us
    unnamed x21, local copies, waits for them, and re-layouts  12.2 us
    ppermute x4, starting transfers between devices, gather_around(): from_left = lax.ppermute(from_left, axis, right)  11.7 us
    all_to_all x1, waiting for transfers between devices, body(): lax.all_to_all(first_kernel, 'section', split_axis=1, concat_axis=2, tile...  8.03 us
    gather x6, local copies, waits for them, and re-layouts, add_offset(): jnp.take(every_id, clipped, axis=0) == session_list  7.59 us
    ppermute x2, starting transfers between devices, gather_around(): from_right = lax.ppermute(from_right, axis, left)  6.36 us
  transfers between devices with their start and end apart: 9, of which 5 were waited for; matrix products, arithmetic and copies ran while one was open for 17% of the time, Pallas kernels for 0%

profile of v1, /device:TPU:8, one launch (start us, length us, event | category | flops | bytes accessed | tf_op | source)
XLA Modules:
  0.0 177.5 jit_solution(13010133923192974474)
XLA Ops:
  0.0 4.1 %copy.52 = bf16[3,1024,256]{2,0,1:T(4,128)(2,1)} copy(bf16[3,1024,256]{2,1,0:T(8,128)(2,1)} %param.14) | data formatting | bytes 3145728 | tf_op args[5]
  4.1 4.6 %all-to-all-start = ((bf16[3,1024,256]{2,0,1:T(4,128)(2,1)}), bf16[3,1024,256]{2,0,1:T(4,128)(2,1)}, u32[]{:S(2)}, u32[]{:S(2)}) async-start(bf16[3,1024,256]{2,0,1:T(4,128)(2,1)} %copy.52), calls=%async_computation | async-start | bytes 4194304 | tf_op jit(solution)/shard_map/all_to_all | solution.py:77
  8.9 0.9 copy.51
  10.0 1.9 %constant_dynamic-update-slice_fusion.7 = (bf16[1024,2,256]{0,2,1:T(8,128)(2,1)S(1)}, bf16[256,2,256]{0,2,1:T(8,128)(2,1)}) fusion(bf16[1024,2,256]{0,2,1:T(8,128)(2,1)S(1)} %broadcast.155.clone, s32[]{:T(128)S(6)} %select_n.94, bf16[256,2,256]{0,2,1:T(8,128)(2,1)} %copy.51, bf16[256,2,256]{0,2,1:T(8,128)(2,1)S(1)} %copy.50), kind=kLoop, calls=%fused_computation.66 | loop fusion | flops 1572864 | bytes 1048580 | tf_op jit(solution)/shard_map/dynamic_update_slice | solution.py:17
  11.9 3.9 %collective-permute-start = (bf16[256,2,256]{0,2,1:T(8,128)(2,1)}, bf16[256,2,256]{0,2,1:T(8,128)(2,1)}, u32[]{:S(2)}, u32[]{:S(2)}) collective-permute-start(bf16[256,2,256]{0,2,1:T(8,128)(2,1)} %get-tuple-element.150), channel_id=1, source_target_pairs={{0,128},{128,256},{256,384},{384,0},{1,129},{129,257},{257,385},{3... | collective-permute-start | bytes 786440 | tf_op jit(solution)/shard_map/ppermute | solution.py:21
  15.7 3.2 %collective-permute-start.1 = (bf16[256,2,256]{0,2,1:T(8,128)(2,1)}, bf16[256,2,256]{0,2,1:T(8,128)(2,1)}, u32[]{:S(2)}, u32[]{:S(2)}) collective-permute-start(bf16[256,2,256]{0,2,1:T(8,128)(2,1)} %get-tuple-element.150), channel_id=1, source_target_pairs={{0,384},{128,0},{256,128},{384,256},{1,385},{129,1},{257,129},{385... | collective-permute-start | bytes 786440 | tf_op jit(solution)/shard_map/ppermute | solution.py:26
  18.9 21.8 %collective-permute-done = bf16[256,2,256]{0,2,1:T(8,128)(2,1)} collective-permute-done((bf16[256,2,256]{0,2,1:T(8,128)(2,1)}, bf16[256,2,256]{0,2,1:T(8,128)(2,1)}, u32[]{:S(2)}, u32[]{:S(2)}) %collective-permute-start) | collective-permute-done | bytes 262176 | tf_op jit(solution)/shard_map/ppermute | solution.py:21
  40.7 1.9 %collective-permute-start.2 = (bf16[256,2,256]{0,2,1:T(8,128)(2,1)}, bf16[256,2,256]{0,2,1:T(8,128)(2,1)}, u32[]{:S(2)}, u32[]{:S(2)}) collective-permute-start(bf16[256,2,256]{0,2,1:T(8,128)(2,1)} %collective-permute-done), channel_id=1, source_target_pairs={{0,128},{128,256},{256,384},{384,0},{1,129},{129,257},{257,385},{3... | collective-permute-start | bytes 786440 | tf_op jit(solution)/shard_map/ppermute | solution.py:21
  42.7 1.8 %copy.54 = bf16[256,2,256]{0,2,1:T(8,128)(2,1)} copy(bf16[256,2,256]{2,1,0:T(2,128)(2,1)} %param.10) | data formatting | bytes 524288 | tf_op args[1]
  44.5 2.7 %copy.55 = bf16[3,1024,256]{2,0,1:T(4,128)(2,1)} copy(bf16[3,1024,256]{2,1,0:T(8,128)(2,1)S(1)} %copy-done.2) | data formatting | bytes 3145728 | tf_op args[4]
  47.2 1.0 constant_dynamic-update-slice_fusion.6
  48.2 1.0 constant_dynamic-update-slice_fusion.5
  49.2 2.1 %collective-permute-done.2 = bf16[256,2,256]{0,2,1:T(8,128)(2,1)} collective-permute-done((bf16[256,2,256]{0,2,1:T(8,128)(2,1)}, bf16[256,2,256]{0,2,1:T(8,128)(2,1)}, u32[]{:S(2)}, u32[]{:S(2)}) %collective-permute-start.2) | collective-permute-done | bytes 262176 | tf_op jit(solution)/shard_map/ppermute | solution.py:21
  51.3 1.0 constant_dynamic-update-slice_fusion.4
  52.3 4.5 %all-to-all-start.1 = ((bf16[3,1024,256]{2,0,1:T(4,128)(2,1)}), bf16[3,1024,256]{2,0,1:T(4,128)(2,1)}, u32[]{:S(2)}, u32[]{:S(2)}) async-start(bf16[3,1024,256]{2,0,1:T(4,128)(2,1)} %copy.55), calls=%async_computation.1 | async-start | bytes 4194304 | tf_op jit(solution)/shard_map/all_to_all | solution.py:76
  56.8 3.1 %copy.79 = bf16[3,4,256,256]{3,1,2,0:T(4,128)(2,1)S(1)} copy(bf16[3,4,256,256]{3,0,2,1:T(4,128)(2,1)} %bitcast.1) | data formatting | bytes 3145728 | tf_op jit(solution)/shard_map/all_to_all | solution.py:77
  60.4 1.2 reshape.105
  61.6 1.5 convolution_bitcast_fusion.4
  65.5 1.2 reshape.104
  66.8 2.6 %constant_dynamic-update-slice_fusion.3 = (bf16[1024,2,256]{0,2,1:T(8,128)(2,1)S(1)}, bf16[256,2,256]{0,2,1:T(8,128)(2,1)}, f32[256,2,256]{0,2,1:T(8,128)}) fusion(bf16[1024,2,256]{0,2,1:T(8,128)(2,1)S(1)} %broadcast.155, s32[]{:T(128)S(6)} %select_n.94, bf16[256,2,256]{0,2,1:T(8,128)(2,1)} %copy.54, f32[256,2,128]{0,2,1:T(8,128)} %slice.54, ...), kind=kOutput, calls=%fused_computation.62 | convolution fusion | flops 270663680 | bytes 3801092 | tf_op jit(solution)/shard_map/dot_general | solution.py:48
  69.4 3.9 %collective-permute-start.3 = (bf16[256,2,256]{0,2,1:T(8,128)(2,1)}, bf16[256,2,256]{0,2,1:T(8,128)(2,1)S(1)}, u32[]{:S(2)}, u32[]{:S(2)}) collective-permute-start(bf16[256,2,256]{0,2,1:T(8,128)(2,1)} %get-tuple-element.148), channel_id=1, source_target_pairs={{0,128},{128,256},{256,384},{384,0},{1,129},{129,257},{257,385},{3... | collective-permute-start | bytes 786440 | tf_op jit(solution)/shard_map/ppermute | solution.py:21
  73.3 3.2 %collective-permute-start.4 = (bf16[256,2,256]{0,2,1:T(8,128)(2,1)}, bf16[256,2,256]{0,2,1:T(8,128)(2,1)}, u32[]{:S(2)}, u32[]{:S(2)}) collective-permute-start(bf16[256,2,256]{0,2,1:T(8,128)(2,1)} %get-tuple-element.148), channel_id=1, source_target_pairs={{0,384},{128,0},{256,128},{384,256},{1,385},{129,1},{257,129},{385... | collective-permute-start | bytes 786440 | tf_op jit(solution)/shard_map/ppermute | solution.py:26
  76.5 8.0 %all-to-all-done.1 = bf16[3,1024,256]{2,0,1:T(4,128)(2,1)} async-done(((bf16[3,1024,256]{2,0,1:T(4,128)(2,1)}), bf16[3,1024,256]{2,0,1:T(4,128)(2,1)}, u32[]{:S(2)}, u32[]{:S(2)}) %all-to-all-start.1) | async-done | bytes 1572896 | tf_op jit(solution)/shard_map/all_to_all | solution.py:76
  84.5 1.8 %copy.56 = bf16[3,1024,256]{2,1,0:T(8,128)(2,1)S(1)} copy(bf16[3,1024,256]{2,0,1:T(4,128)(2,1)} %all-to-all-done.1) | data formatting | bytes 3145728 | tf_op jit(solution)/shard_map/all_to_all | solution.py:76
  86.3 0.8 collective-permute-done.3
  87.1 2.1 %collective-permute-start.5 = (bf16[256,2,256]{0,2,1:T(8,128)(2,1)S(1)}, bf16[256,2,256]{0,2,1:T(8,128)(2,1)}, u32[]{:S(2)}, u32[]{:S(2)}) collective-permute-start(bf16[256,2,256]{0,2,1:T(8,128)(2,1)S(1)} %collective-permute-done.3), channel_id=1, source_target_pairs={{0,128},{128,256},{256,384},{384,0},{1,129},{129,257},{257,385},{3... | collective-permute-start | bytes 786440 | tf_op jit(solution)/shard_map/ppermute | solution.py:21
  89.2 0.9 fusion.35
  90.6 1.2 copy.57
  91.9 1.0 constant_dynamic-update-slice_fusion.1
  92.8 5.7 %collective-permute-done.5 = bf16[256,2,256]{0,2,1:T(8,128)(2,1)} collective-permute-done((bf16[256,2,256]{0,2,1:T(8,128)(2,1)S(1)}, bf16[256,2,256]{0,2,1:T(8,128)(2,1)}, u32[]{:S(2)}, u32[]{:S(2)}) %collective-permute-start.5) | collective-permute-done | bytes 262176 | tf_op jit(solution)/shard_map/ppermute | solution.py:21
  98.6 1.0 constant_dynamic-update-slice_fusion
  100.5 2.0 %fusion.3 = bf16[128,2,4,256]{0,3,2,1:T(8,128)(2,1)S(1)} fusion(f32[256,2,256]{0,2,1:T(8,128)} %get-tuple-element.157, bf16[1024,2,256]{0,2,1:T(8,128)(2,1)S(1)} %constant_dynamic-update-slice_fusion, bf16[256,1024,1]{0,1,2:T(8,128)(2,1)S(1)} %bitcast.89, bf16[128,4,2,256]{3,2,1,0:T(2,128)(2,1)S(1)} %bitcast.84, f32[256,2,192]{0,2,1:T(8,128)S(1)} %slice.59, ...), kind=kOutput, calls=%fused_computation.13 | convolution fusion | flops 403439616 | bytes 3997696 | tf_op jit(solution)/shard_map/jbil,cil->jibc/dot_general | solution.py:88
  102.5 1.2 copy.65
  103.7 19.5 %all-to-all-start.2 = ((bf16[128,2,4,256]{3,2,1,0:T(4,128)(2,1)}), bf16[128,2,4,256]{3,2,1,0:T(4,128)(2,1)S(1)}, u32[]{:S(2)}, u32[]{:S(2)}) async-start(bf16[128,2,4,256]{3,2,1,0:T(4,128)(2,1)} %copy.65), calls=%async_computation.2 | async-start | bytes 1048576 | tf_op jit(solution)/shard_map/all_to_all | solution.py:91
  123.3 1.3 dynamic-slice
  125.5 37.0 %all-reduce.4 = s32[256]{0:T(256)S(1)} all-reduce(s32[256]{0:T(256)S(1)} %dynamic-update-slice), channel_id=1, replica_groups=mesh['section'=4,'trial'=128] {'trial'}, use_global_device_ids=true, to_apply=%add.4 | all-reduce | flops 256 | bytes 2048
  162.8 13.8 %while.14 = (s32[]{:T(128)}, f32[128,1024]{1,0:T(8,128)S(1)}, s32[128]{0:T(128)S(1)}, s32[256]{0:T(256)S(1)}, f32[256,1024]{1,0:T(8,128)S(1)}, /*index=5*/s32[]{:T(128)}, s32[]{:T(128)}) while((s32[]{:T(128)}, f32[128,1024]{1,0:T(8,128)S(1)}, s32[128]{0:T(128)S(1)}, s32[256]{0:T(256)S(1)}, f32[256,1024]{1,0:T(8,128)S(1)}, ...), condition=%wide.region_2.3_spmd.clone, body=%wide.region_1.2_spmd.clone.sunk | while | flops 527491 | bytes 2630751 | solution.py:108
  162.8 1.3 gather_fusion.1
  164.1 0.8 gather_fusion
  165.1 1.3 gather_fusion.1
  167.4 1.3 gather_fusion.1
  168.7 0.8 gather_fusion
  169.7 1.3 gather_fusion.1
  171.0 0.8 gather_fusion
  172.0 1.3 gather_fusion.1
  173.3 0.8 gather_fusion
  174.3 1.3 gather_fusion.1
  176.6 0.9 convert_element_type.61
  (64 shorter events, 7.9 us)
Async XLA Ops:
  0.0 100.5 %copy-start = (bf16[512,2,256]{2,1,0:T(2,128)(2,1)S(1)}, bf16[512,2,256]{2,1,0:T(2,128)(2,1)}, u32[]{:S(2)}) copy-start(bf16[512,2,256]{2,1,0:T(2,128)(2,1)} %param.9) | copy-start | bytes 1572868
  4.1 4.6 %copy-start.3 = (bf16[256,2,256]{2,1,0:T(2,128)(2,1)S(1)}, bf16[256,2,256]{2,1,0:T(2,128)(2,1)}, u32[]{:S(2)}) copy-start(bf16[256,2,256]{2,1,0:T(2,128)(2,1)} %param.12) | copy-start | bytes 786436
  4.1 4.8 %copy-start.4 = (bf16[256,2,256]{2,1,0:T(2,128)(2,1)S(1)}, bf16[256,2,256]{2,1,0:T(2,128)(2,1)}, u32[]{:S(2)}) copy-start(bf16[256,2,256]{2,1,0:T(2,128)(2,1)} %param.11) | copy-start | bytes 786436
  4.1 48.2 %all-to-all-start = ((bf16[3,1024,256]{2,0,1:T(4,128)(2,1)}), bf16[3,1024,256]{2,0,1:T(4,128)(2,1)}, u32[]{:S(2)}, u32[]{:S(2)}) async-start(bf16[3,1024,256]{2,0,1:T(4,128)(2,1)} %copy.52), calls=%async_computation | async-start | bytes 4194304 | tf_op jit(solution)/shard_map/all_to_all | solution.py:77
  8.9 35.6 %copy-start.2 = (bf16[3,1024,256]{2,1,0:T(8,128)(2,1)S(1)}, bf16[3,1024,256]{2,1,0:T(8,128)(2,1)}, u32[]{:S(2)}) copy-start(bf16[3,1024,256]{2,1,0:T(8,128)(2,1)} %param.13) | copy-start | bytes 4718596
  11.9 28.9 %collective-permute-start = (bf16[256,2,256]{0,2,1:T(8,128)(2,1)}, bf16[256,2,256]{0,2,1:T(8,128)(2,1)}, u32[]{:S(2)}, u32[]{:S(2)}) collective-permute-start(bf16[256,2,256]{0,2,1:T(8,128)(2,1)} %get-tuple-element.150), channel_id=1, source_target_pairs={{0,128},{128,256},{256,384},{384,0},{1,129},{129,257},{257,385},{3... | collective-permute-start | bytes 786440 | tf_op jit(solution)/shard_map/ppermute | solution.py:21
  15.7 32.4 %collective-permute-start.1 = (bf16[256,2,256]{0,2,1:T(8,128)(2,1)}, bf16[256,2,256]{0,2,1:T(8,128)(2,1)}, u32[]{:S(2)}, u32[]{:S(2)}) collective-permute-start(bf16[256,2,256]{0,2,1:T(8,128)(2,1)} %get-tuple-element.150), channel_id=1, source_target_pairs={{0,384},{128,0},{256,128},{384,256},{1,385},{129,1},{257,129},{385... | collective-permute-start | bytes 786440 | tf_op jit(solution)/shard_map/ppermute | solution.py:26
  40.7 10.6 %collective-permute-start.2 = (bf16[256,2,256]{0,2,1:T(8,128)(2,1)}, bf16[256,2,256]{0,2,1:T(8,128)(2,1)}, u32[]{:S(2)}, u32[]{:S(2)}) collective-permute-start(bf16[256,2,256]{0,2,1:T(8,128)(2,1)} %collective-permute-done), channel_id=1, source_target_pairs={{0,128},{128,256},{256,384},{384,0},{1,129},{129,257},{257,385},{3... | collective-permute-start | bytes 786440 | tf_op jit(solution)/shard_map/ppermute | solution.py:21
  52.3 32.2 %all-to-all-start.1 = ((bf16[3,1024,256]{2,0,1:T(4,128)(2,1)}), bf16[3,1024,256]{2,0,1:T(4,128)(2,1)}, u32[]{:S(2)}, u32[]{:S(2)}) async-start(bf16[3,1024,256]{2,0,1:T(4,128)(2,1)} %copy.55), calls=%async_computation.1 | async-start | bytes 4194304 | tf_op jit(solution)/shard_map/all_to_all | solution.py:76
  63.1 0.8 copy-start.1
  64.7 2.0 %slice-start = ((f32[256,2,256]{0,2,1:T(8,128)}), f32[256,2,192]{0,2,1:T(8,128)S(1)}, s32[]{:S(2)}) async-start(f32[256,2,256]{0,2,1:T(8,128)} %copy-done.1), calls=%async_computation.3 | async-start | bytes 786432 | tf_op jit(solution)/shard_map/slice | solution.py:42
  69.4 17.7 %collective-permute-start.3 = (bf16[256,2,256]{0,2,1:T(8,128)(2,1)}, bf16[256,2,256]{0,2,1:T(8,128)(2,1)S(1)}, u32[]{:S(2)}, u32[]{:S(2)}) collective-permute-start(bf16[256,2,256]{0,2,1:T(8,128)(2,1)} %get-tuple-element.148), channel_id=1, source_target_pairs={{0,128},{128,256},{256,384},{384,0},{1,129},{129,257},{257,385},{3... | collective-permute-start | bytes 786440 | tf_op jit(solution)/shard_map/ppermute | solution.py:21
  73.3 18.6 %collective-permute-start.4 = (bf16[256,2,256]{0,2,1:T(8,128)(2,1)}, bf16[256,2,256]{0,2,1:T(8,128)(2,1)}, u32[]{:S(2)}, u32[]{:S(2)}) collective-permute-start(bf16[256,2,256]{0,2,1:T(8,128)(2,1)} %get-tuple-element.148), channel_id=1, source_target_pairs={{0,384},{128,0},{256,128},{384,256},{1,385},{129,1},{257,129},{385... | collective-permute-start | bytes 786440 | tf_op jit(solution)/shard_map/ppermute | solution.py:26
  87.1 11.4 %collective-permute-start.5 = (bf16[256,2,256]{0,2,1:T(8,128)(2,1)S(1)}, bf16[256,2,256]{0,2,1:T(8,128)(2,1)}, u32[]{:S(2)}, u32[]{:S(2)}) collective-permute-start(bf16[256,2,256]{0,2,1:T(8,128)(2,1)S(1)} %collective-permute-done.3), channel_id=1, source_target_pairs={{0,128},{128,256},{256,384},{384,0},{1,129},{129,257},{257,385},{3... | collective-permute-start | bytes 786440 | tf_op jit(solution)/shard_map/ppermute | solution.py:21
  102.5 22.7 %copy-start.5 = (s32[2]{0:T(128)S(1)}, s32[2]{0:T(128)}, u32[]{:S(2)}) copy-start(s32[2]{0:T(128)} %param.15) | copy-start | bytes 28
  103.7 58.9 %all-to-all-start.2 = ((bf16[128,2,4,256]{3,2,1,0:T(4,128)(2,1)}), bf16[128,2,4,256]{3,2,1,0:T(4,128)(2,1)S(1)}, u32[]{:S(2)}, u32[]{:S(2)}) async-start(bf16[128,2,4,256]{3,2,1,0:T(4,128)(2,1)} %copy.65), calls=%async_computation.2 | async-start | bytes 1048576 | tf_op jit(solution)/shard_map/all_to_all | solution.py:91
